TPU v7x, 32 devices: a whole 2x2x4 slice. The times are simulated.
32 devices in a mesh: blade: 4 (over z), inst: 4 (over x, core), cell: 2 (over y).
Axes of the slice: x: 2, y: 2, z: 4, core: 2. Of those that a mesh axis runs over, the one named last changes fastest.
Arguments:
- cell_coords: float32 [3, 320, 512], P(None, ('blade', 'cell'), 'inst'), may hold values from 0 to 1
- centre_points: float32 [3, 4096], P(None, ('blade', 'inst', 'cell')), may hold values from 0 to 1
- coefficients: float32 [24, 4096], P(None, ('blade', 'inst', 'cell')), may hold values from -1.2 to 1.2
- tile_lists: int32 [320, 4, 4], P(('blade', 'cell'), 'inst'), may hold values from 0 to 31, as said below
Outputs:
- displaced: float32 [8, 3, 320, 512], P('inst', None, ('blade', 'cell'))
- grid_velocity: float32 [8, 3, 320, 512], P('inst', None, ('blade', 'cell'))
Inputs may be any that keep to these rules, and one draw needn't show every extreme that they name: `tile_lists`: entry k of every list lies in k * 8 to (k + 1) * 8 - 1, so each cell tile draws centre tiles from every blade.
All inputs are finite; a program needn't handle non-finite values.
Results may differ from a plain program's by a relative error of at most 0.0003.
Values sent between devices are 32-bit elements; how exact they have to be, the bound alone decides.
No kernel may reach another device: no remote copies, remote signals or barrier semaphores. Data moves between devices by JAX's collectives and lax.ppermute only.
A program may use at most 64 MiB of HBM per device.

v0:
```python
import jax
import jax.numpy as jnp
from jax import lax
from jax.sharding import PartitionSpec as P

NT = 8
TILE = 128


def wendland(cell_tiles, near_points):
    squared = jnp.zeros(near_points.shape[1:] + cell_tiles.shape[-1:], jnp.float32)
    for axis_id in range(3):
        offset = near_points[axis_id][..., :, None] - cell_tiles[axis_id][:, None, None, :]
        squared = squared + offset * offset
    scaled = jnp.sqrt(squared) / 0.4
    margin = jnp.maximum(1.0 - scaled, 0.0)
    margin_sq = margin * margin
    return margin_sq * margin_sq * (1.0 + 4.0 * scaled)


def tile_sums(cell_tiles, list_rows, point_tiles, coef_tiles):
    near_points = point_tiles[:, list_rows]
    near_coefs = coef_tiles[:, list_rows]
    weights = wendland(cell_tiles, near_points)
    return jnp.einsum("amkj,mkjc->amc", near_coefs, weights, precision=lax.Precision.HIGHEST)


def block_sums(cell_tiles, list_rows, point_tiles, coef_tiles, width):
    groups = cell_tiles.shape[1] // width
    cell_groups = jnp.moveaxis(cell_tiles.reshape(3, groups, width, cell_tiles.shape[2]), 1, 0)
    list_groups = list_rows.reshape(groups, width, list_rows.shape[1])

    def one_group(operands):
        return tile_sums(operands[0], operands[1], point_tiles, coef_tiles)

    tile_totals = lax.map(one_group, (cell_groups, list_groups))
    return jnp.moveaxis(tile_totals, 0, 1).reshape(
        coef_tiles.shape[0], cell_tiles.shape[1], cell_tiles.shape[2]
    )


def spectral_matrix(instances):
    later = jnp.arange(instances, dtype=jnp.int32)[:, None]
    earlier = jnp.arange(instances, dtype=jnp.int32)[None, :]
    distance = (later - earlier).astype(jnp.float32)
    parity = jnp.where((later - earlier) % 2 == 0, 1.0, -1.0).astype(jnp.float32)
    guarded = jnp.where(distance == 0, 0.5, jnp.pi * distance / instances)
    values = 0.5 * parity * jnp.cos(guarded) / jnp.sin(guarded)
    return jnp.where(distance == 0, 0.0, values)


def on_device(cell_coords, centre_points, coefficients, tile_lists):
    coef_all, point_all = (
        lax.all_gather(coefficients, ("blade", "inst", "cell"), axis=1, tiled=True),
        lax.all_gather(centre_points, ("blade", "inst", "cell"), axis=1, tiled=True),
    )
    point_tiles = point_all.reshape(3, point_all.shape[1] // TILE, TILE)
    coef_tiles = coef_all.reshape(NT * 3, coef_all.shape[1] // TILE, TILE)
    row_count = cell_coords.shape[1]
    matrix = spectral_matrix(NT)
    shift = block_sums(cell_coords, tile_lists[:, 0, :], point_tiles, coef_tiles, 4)
    shift = shift.reshape(NT, 3, row_count, TILE)
    moved_points = cell_coords[None] + shift
    velocity_local = jnp.einsum("ts,sarc->tarc", matrix, shift, precision=lax.Precision.HIGHEST)
    displaced, grid_velocity = (
        lax.all_to_all(moved_points, "inst", split_axis=0, concat_axis=3, tiled=True),
        lax.all_to_all(velocity_local, "inst", split_axis=0, concat_axis=3, tiled=True),
    )
    return (displaced, grid_velocity)


def solution(mesh):
    in_specs = (
        P(None, ("blade", "cell"), "inst"),
        P(None, ("blade", "inst", "cell")),
        P(None, ("blade", "inst", "cell")),
        P(("blade", "cell"), "inst", None),
    )
    out_specs = (P("inst", None, ("blade", "cell"), None), P("inst", None, ("blade", "cell"), None))
    return jax.shard_map(
        on_device, mesh=mesh, in_specs=in_specs, out_specs=out_specs, check_vma=False
    )
```

profile of v0, /device:TPU:0, one launch (start us, length us, event | category | flops | bytes accessed | tf_op | source)
XLA Modules:
  0.0 199.8 jit_solution(7670787411031908554)
XLA Ops:
  0.6 72.0 %all_gather.7 = f32[24,4096]{1,0:T(8,128)S(1)} all-gather(f32[24,128]{1,0:T(8,128)} %param.8), channel_id=1, replica_groups=mesh['blade'=4,'inst'=4,'cell'=2] {'blade','inst','cell'}, dimensions={1}, use_global_device_ids=true | all-gather | bytes 405504 | tf_op jit(solution)/shard_map/all_gather | solution.py:54
  72.7 0.7 copy-done.1
  73.3 63.8 %all_gather.6 = f32[3,4096]{1,0:T(4,128)S(1)} all-gather(f32[3,128]{1,0:T(4,128)S(1)} %copy-done.1), channel_id=1, replica_groups=mesh['blade'=4,'inst'=4,'cell'=2] {'blade','inst','cell'}, dimensions={1}, use_global_device_ids=true | all-gather | bytes 50688 | tf_op jit(solution)/shard_map/all_gather | solution.py:55
  137.2 36.3 %while.12 = (s32[]{:T(128)}, f32[10,24,4,128]{3,1,2,0:T(8,128)S(1)}, s32[10,4,4]{2,1,0:T(4,128)S(1)}, f32[3,32,128]{2,0,1:T(4,128)S(1)}, f32[10,3,4,128]{3,2,0,1...) while((s32[]{:T(128)}, f32[10,24,4,128]{3,1,2,0:T(8,128)S(1)}, s32[10,4,4]{2,1,0:T(4,128)S(1)}, ...), condition=%wide.region_1.2_spmd, body=%wide.region_0.1_spmd.sunk | while | flops 79692848 | bytes 797209 | solution.py:36
  137.3 0.6 gather_fusion.1
  138.5 2.3 %fusion.79 = f32[10,24,4,128]{3,1,2,0:T(8,128)S(1)} fusion(f32[10,24,4,128]{3,1,2,0:T(8,128)S(1)} %get-tuple-element.173, s32[]{:T(128)} %get-tuple-element.172, f32[24,4,4,128]{3,0,2,1:T(8,128)S(1)} %bitcast.82, f32[4,128]{1,0:T(4,128)S(1)} %get-tuple-element.159, f32[4,4,128]{2,1,0:T(4,128)S(1)} %bitcast.94, f32[4,128]{1,0:T(4,128)S(1)} %get-tuple-element.161, ...), kind=kOutput, calls=%fused_computation.3.clone.1 | convolution fusion | flops 79691776 | bytes 276484 | tf_op jit(solution)/shard_map/while/body/eval_jaxpr/amkj,mkjc->amc/dot_general | solution.py:25
  141.0 0.6 gather_fusion.1
  142.2 2.3 %fusion.79 = f32[10,24,4,128]{3,1,2,0:T(8,128)S(1)} fusion(f32[10,24,4,128]{3,1,2,0:T(8,128)S(1)} %get-tuple-element.173, s32[]{:T(128)} %get-tuple-element.172, f32[24,4,4,128]{3,0,2,1:T(8,128)S(1)} %bitcast.82, f32[4,128]{1,0:T(4,128)S(1)} %get-tuple-element.159, f32[4,4,128]{2,1,0:T(4,128)S(1)} %bitcast.94, f32[4,128]{1,0:T(4,128)S(1)} %get-tuple-element.161, ...), kind=kOutput, calls=%fused_computation.3.clone.1 | convolution fusion | flops 79691776 | bytes 276484 | tf_op jit(solution)/shard_map/while/body/eval_jaxpr/amkj,mkjc->amc/dot_general | solution.py:25
  144.6 0.6 gather_fusion.1
  145.8 2.3 %fusion.79 = f32[10,24,4,128]{3,1,2,0:T(8,128)S(1)} fusion(f32[10,24,4,128]{3,1,2,0:T(8,128)S(1)} %get-tuple-element.173, s32[]{:T(128)} %get-tuple-element.172, f32[24,4,4,128]{3,0,2,1:T(8,128)S(1)} %bitcast.82, f32[4,128]{1,0:T(4,128)S(1)} %get-tuple-element.159, f32[4,4,128]{2,1,0:T(4,128)S(1)} %bitcast.94, f32[4,128]{1,0:T(4,128)S(1)} %get-tuple-element.161, ...), kind=kOutput, calls=%fused_computation.3.clone.1 | convolution fusion | flops 79691776 | bytes 276484 | tf_op jit(solution)/shard_map/while/body/eval_jaxpr/amkj,mkjc->amc/dot_general | solution.py:25
  148.2 0.6 gather_fusion.1
  149.4 2.3 %fusion.79 = f32[10,24,4,128]{3,1,2,0:T(8,128)S(1)} fusion(f32[10,24,4,128]{3,1,2,0:T(8,128)S(1)} %get-tuple-element.173, s32[]{:T(128)} %get-tuple-element.172, f32[24,4,4,128]{3,0,2,1:T(8,128)S(1)} %bitcast.82, f32[4,128]{1,0:T(4,128)S(1)} %get-tuple-element.159, f32[4,4,128]{2,1,0:T(4,128)S(1)} %bitcast.94, f32[4,128]{1,0:T(4,128)S(1)} %get-tuple-element.161, ...), kind=kOutput, calls=%fused_computation.3.clone.1 | convolution fusion | flops 79691776 | bytes 276484 | tf_op jit(solution)/shard_map/while/body/eval_jaxpr/amkj,mkjc->amc/dot_general | solution.py:25
  151.8 0.6 gather_fusion.1
  153.1 2.3 %fusion.79 = f32[10,24,4,128]{3,1,2,0:T(8,128)S(1)} fusion(f32[10,24,4,128]{3,1,2,0:T(8,128)S(1)} %get-tuple-element.173, s32[]{:T(128)} %get-tuple-element.172, f32[24,4,4,128]{3,0,2,1:T(8,128)S(1)} %bitcast.82, f32[4,128]{1,0:T(4,128)S(1)} %get-tuple-element.159, f32[4,4,128]{2,1,0:T(4,128)S(1)} %bitcast.94, f32[4,128]{1,0:T(4,128)S(1)} %get-tuple-element.161, ...), kind=kOutput, calls=%fused_computation.3.clone.1 | convolution fusion | flops 79691776 | bytes 276484 | tf_op jit(solution)/shard_map/while/body/eval_jaxpr/amkj,mkjc->amc/dot_general | solution.py:25
  155.5 0.6 gather_fusion.1
  156.7 2.3 %fusion.79 = f32[10,24,4,128]{3,1,2,0:T(8,128)S(1)} fusion(f32[10,24,4,128]{3,1,2,0:T(8,128)S(1)} %get-tuple-element.173, s32[]{:T(128)} %get-tuple-element.172, f32[24,4,4,128]{3,0,2,1:T(8,128)S(1)} %bitcast.82, f32[4,128]{1,0:T(4,128)S(1)} %get-tuple-element.159, f32[4,4,128]{2,1,0:T(4,128)S(1)} %bitcast.94, f32[4,128]{1,0:T(4,128)S(1)} %get-tuple-element.161, ...), kind=kOutput, calls=%fused_computation.3.clone.1 | convolution fusion | flops 79691776 | bytes 276484 | tf_op jit(solution)/shard_map/while/body/eval_jaxpr/amkj,mkjc->amc/dot_general | solution.py:25
  159.1 0.6 gather_fusion.1
  160.3 2.3 %fusion.79 = f32[10,24,4,128]{3,1,2,0:T(8,128)S(1)} fusion(f32[10,24,4,128]{3,1,2,0:T(8,128)S(1)} %get-tuple-element.173, s32[]{:T(128)} %get-tuple-element.172, f32[24,4,4,128]{3,0,2,1:T(8,128)S(1)} %bitcast.82, f32[4,128]{1,0:T(4,128)S(1)} %get-tuple-element.159, f32[4,4,128]{2,1,0:T(4,128)S(1)} %bitcast.94, f32[4,128]{1,0:T(4,128)S(1)} %get-tuple-element.161, ...), kind=kOutput, calls=%fused_computation.3.clone.1 | convolution fusion | flops 79691776 | bytes 276484 | tf_op jit(solution)/shard_map/while/body/eval_jaxpr/amkj,mkjc->amc/dot_general | solution.py:25
  163.9 2.3 %fusion.79 = f32[10,24,4,128]{3,1,2,0:T(8,128)S(1)} fusion(f32[10,24,4,128]{3,1,2,0:T(8,128)S(1)} %get-tuple-element.173, s32[]{:T(128)} %get-tuple-element.172, f32[24,4,4,128]{3,0,2,1:T(8,128)S(1)} %bitcast.82, f32[4,128]{1,0:T(4,128)S(1)} %get-tuple-element.159, f32[4,4,128]{2,1,0:T(4,128)S(1)} %bitcast.94, f32[4,128]{1,0:T(4,128)S(1)} %get-tuple-element.161, ...), kind=kOutput, calls=%fused_computation.3.clone.1 | convolution fusion | flops 79691776 | bytes 276484 | tf_op jit(solution)/shard_map/while/body/eval_jaxpr/amkj,mkjc->amc/dot_general | solution.py:25
  166.4 0.6 gather_fusion.1
  167.6 2.3 %fusion.79 = f32[10,24,4,128]{3,1,2,0:T(8,128)S(1)} fusion(f32[10,24,4,128]{3,1,2,0:T(8,128)S(1)} %get-tuple-element.173, s32[]{:T(128)} %get-tuple-element.172, f32[24,4,4,128]{3,0,2,1:T(8,128)S(1)} %bitcast.82, f32[4,128]{1,0:T(4,128)S(1)} %get-tuple-element.159, f32[4,4,128]{2,1,0:T(4,128)S(1)} %bitcast.94, f32[4,128]{1,0:T(4,128)S(1)} %get-tuple-element.161, ...), kind=kOutput, calls=%fused_computation.3.clone.1 | convolution fusion | flops 79691776 | bytes 276484 | tf_op jit(solution)/shard_map/while/body/eval_jaxpr/amkj,mkjc->amc/dot_general | solution.py:25
  170.0 0.6 gather_fusion.1
  171.2 2.3 %fusion.79 = f32[10,24,4,128]{3,1,2,0:T(8,128)S(1)} fusion(f32[10,24,4,128]{3,1,2,0:T(8,128)S(1)} %get-tuple-element.173, s32[]{:T(128)} %get-tuple-element.172, f32[24,4,4,128]{3,0,2,1:T(8,128)S(1)} %bitcast.82, f32[4,128]{1,0:T(4,128)S(1)} %get-tuple-element.159, f32[4,4,128]{2,1,0:T(4,128)S(1)} %bitcast.94, f32[4,128]{1,0:T(4,128)S(1)} %get-tuple-element.161, ...), kind=kOutput, calls=%fused_computation.3.clone.1 | convolution fusion | flops 79691776 | bytes 276484 | tf_op jit(solution)/shard_map/while/body/eval_jaxpr/amkj,mkjc->amc/dot_general | solution.py:25
  173.6 0.6 fusion.32
  174.2 0.9 copy.29
  175.1 3.5 %all-to-all-start.1 = ((f32[8,3,40,128]{3,2,1,0:T(8,128)}), f32[8,3,40,128]{3,2,1,0:T(8,128)S(1)}, u32[]{:S(2)}, u32[]{:S(2)}) async-start(f32[8,3,40,128]{3,2,1,0:T(8,128)} %copy.29), calls=%async_computation.1 | async-start | bytes 983040 | tf_op jit(solution)/shard_map/all_to_all | solution.py:67
  178.6 0.8 broadcast_add_fusion
  179.4 7.6 %all-to-all-done.1 = f32[8,3,40,128]{3,2,1,0:T(8,128)S(1)} async-done(((f32[8,3,40,128]{3,2,1,0:T(8,128)}), f32[8,3,40,128]{3,2,1,0:T(8,128)S(1)}, u32[]{:S(2)}, u32[]{:S(2)}) %all-to-all-start.1) | async-done | bytes 491552 | tf_op jit(solution)/shard_map/all_to_all | solution.py:67
  187.0 3.5 %all-to-all-start = ((f32[8,3,40,128]{3,2,1,0:T(8,128)}), f32[8,3,40,128]{3,2,1,0:T(8,128)S(1)}, u32[]{:S(2)}, u32[]{:S(2)}) async-start(f32[8,3,40,128]{3,2,1,0:T(8,128)} %broadcast_add_fusion), calls=%async_computation | async-start | bytes 983040 | tf_op jit(solution)/shard_map/all_to_all | solution.py:66
  190.5 0.8 copy.42
  191.3 7.6 %all-to-all-done = f32[8,3,40,128]{3,2,1,0:T(8,128)S(1)} async-done(((f32[8,3,40,128]{3,2,1,0:T(8,128)}), f32[8,3,40,128]{3,2,1,0:T(8,128)S(1)}, u32[]{:S(2)}, u32[]{:S(2)}) %all-to-all-start) | async-done | bytes 491552 | tf_op jit(solution)/shard_map/all_to_all | solution.py:66
  198.9 0.8 copy.43
  (80 shorter events, 7.8 us)
Async XLA Ops:
  72.7 0.7 copy-start.1
  73.3 63.8 %copy-start.2 = (s32[40,1,4]{0,2,1:T(4,128)S(1)}, s32[40,1,4]{0,2,1:T(4,128)}, u32[]{:S(2)}) copy-start(s32[40,1,4]{0,2,1:T(4,128)} %param.9) | copy-start | bytes 1924
  73.3 63.9 %copy-start = (f32[3,40,128]{2,1,0:T(8,128)S(1)}, f32[3,40,128]{2,1,0:T(8,128)}, u32[]{:S(2)}) copy-start(f32[3,40,128]{2,1,0:T(8,128)} %param.6) | copy-start | bytes 184324
  175.1 11.9 %all-to-all-start.1 = ((f32[8,3,40,128]{3,2,1,0:T(8,128)}), f32[8,3,40,128]{3,2,1,0:T(8,128)S(1)}, u32[]{:S(2)}, u32[]{:S(2)}) async-start(f32[8,3,40,128]{3,2,1,0:T(8,128)} %copy.29), calls=%async_computation.1 | async-start | bytes 983040 | tf_op jit(solution)/shard_map/all_to_all | solution.py:67
  187.0 11.9 %all-to-all-start = ((f32[8,3,40,128]{3,2,1,0:T(8,128)}), f32[8,3,40,128]{3,2,1,0:T(8,128)S(1)}, u32[]{:S(2)}, u32[]{:S(2)}) async-start(f32[8,3,40,128]{3,2,1,0:T(8,128)} %broadcast_add_fusion), calls=%async_computation | async-start | bytes 983040 | tf_op jit(solution)/shard_map/all_to_all | solution.py:66
where the time goes:
time: 200 us
  blocking collectives  136 us (68%)
  matrix products  23.4 us (12%)
  local copies, waits for them, and re-layouts  16.1 us (8%)
  waiting for transfers between devices  15.2 us (8%)
  starting transfers between devices  6.94 us (3%)
    all_gather x1, blocking collectives, on_device(): lax.all_gather(coefficients, ('blade', 'inst', 'cell'), axis=1, tiled=True)  72 us
    all_gather x1, blocking collectives, on_device(): lax.all_gather(centre_points, ('blade', 'inst', 'cell'), axis=1, tiled=True)  63.8 us
    dot_general x10, matrix products, tile_sums(): jnp.einsum('amkj,mkjc->amc', near_coefs, weights, precision=lax.Precision...  22.8 us
    all_to_all x1, waiting for transfers between devices, on_device(): lax.all_to_all(velocity_local, 'inst', split_axis=0, concat_axis=3, tiled...  7.61 us
    all_to_all x1, waiting for transfers between devices, on_device(): lax.all_to_all(moved_points, 'inst', split_axis=0, concat_axis=3, tiled=T...  7.59 us
    gather x10, local copies, waits for them, and re-layouts, tile_sums(): near_points = point_tiles[:, list_rows]  5.87 us
    gather x10, local copies, waits for them, and re-layouts, tile_sums(): near_coefs = coef_tiles[:, list_rows]  5.66 us
  transfers between devices with their start and end apart: 2, of which 2 were waited for; matrix products, arithmetic and copies ran while one was open for 1% of the time, Pallas kernels for 0%

commit v1 on v0

--- a/solution.py
+++ b/solution.py
@@ -5,6 +5,31 @@
 
 NT = 8
 TILE = 128
+
+
+def cut_along(value, dim, size):
+    before, after = (value.shape[:dim], value.shape[dim + 1 :])
+    return jnp.moveaxis(value.reshape(*before, size, -1, *after), dim, 0)
+
+
+def laid_out(blocks, dim):
+    blocks = jnp.moveaxis(blocks, 0, dim)
+    shape = blocks.shape
+    return blocks.reshape(*shape[:dim], shape[dim] * shape[dim + 1], *shape[dim + 2 :])
+
+
+def exchange_directly(x, axis, split_dim, concat_dim):
+    devices, index = (lax.axis_size(axis), lax.axis_index(axis))
+    blocks = cut_along(x, split_dim, devices)
+    out = blocks
+    for step in range(1, devices):
+        target, source = ((index + step) % devices, (index - step) % devices)
+        sent = lax.dynamic_index_in_dim(blocks, target, 0)
+        partner_block = lax.ppermute(
+            sent, axis, [(i, (i + step) % devices) for i in range(devices)]
+        )
+        out = lax.dynamic_update_slice_in_dim(out, partner_block, source, axis=0)
+    return laid_out(out, concat_dim)
 
 
 def wendland(cell_tiles, near_points):
@@ -63,7 +88,7 @@
     moved_points = cell_coords[None] + shift
     velocity_local = jnp.einsum("ts,sarc->tarc", matrix, shift, precision=lax.Precision.HIGHEST)
     displaced, grid_velocity = (
-        lax.all_to_all(moved_points, "inst", split_axis=0, concat_axis=3, tiled=True),
+        exchange_directly(moved_points, "inst", 0, 3),
         lax.all_to_all(velocity_local, "inst", split_axis=0, concat_axis=3, tiled=True),
     )
     return (displaced, grid_velocity)

time: 200 us -> 194 us (0.970)
  starting transfers between devices: 6.94 us -> 3.65 us
  waiting for transfers between devices: 15.2 us -> 12 us
    all_to_all x1 -> x0, waiting for transfers between devices: 7.59 us -> none  [on_device(): lax.all_to_all(moved_points, 'inst', split_axis=0, concat_axis=3, tiled=T...]
    ppermute x0 -> x3, waiting for transfers between devices: none -> 4.25 us  [exchange_directly(): lax.ppermute(sent, axis, [(i, (i + step) % devices) for i in range(device...]
    all_to_all x1 -> x0, starting transfers between devices: 3.47 us -> none  [on_device(): lax.all_to_all(moved_points, 'inst', split_axis=0, concat_axis=3, tiled=T...]
  transfers between devices with their start and end apart: 2 -> 4, of which waited for: 2 -> 2; matrix products, arithmetic and copies ran while one was open for 1% -> 1% of each run, Pallas kernels for 0% -> 0%
where the time goes in v1:
time: 194 us; the launch traced here: 193 us
  blocking collectives  136 us (70%)
  matrix products  23.4 us (12%)
  local copies, waits for them, and re-layouts  16.9 us (9%)
  waiting for transfers between devices  12 us (6%)
  starting transfers between devices  3.65 us (2%)
    all_gather x1, blocking collectives, on_device(): lax.all_gather(coefficients, ('blade', 'inst', 'cell'), axis=1, tiled=True)  71.8 us
    all_gather x1, blocking collectives, on_device(): lax.all_gather(centre_points, ('blade', 'inst', 'cell'), axis=1, tiled=True)  63.8 us
    dot_general x10, matrix products, tile_sums(): jnp.einsum('amkj,mkjc->amc', near_coefs, weights, precision=lax.Precision...  22.8 us
    all_to_all x1, waiting for transfers between devices, on_device(): lax.all_to_all(velocity_local, 'inst', split_axis=0, concat_axis=3, tiled...  7.8 us
    gather x10, local copies, waits for them, and re-layouts, tile_sums(): near_points = point_tiles[:, list_rows]  5.87 us
    gather x10, local copies, waits for them, and re-layouts, tile_sums(): near_coefs = coef_tiles[:, list_rows]  5.66 us
    ppermute x3, waiting for transfers between devices, exchange_directly(): lax.ppermute(sent, axis, [(i, (i + step) % devices) for i in range(device...  4.25 us
  transfers between devices with their start and end apart: 4, of which 2 were waited for; matrix products, arithmetic and copies ran while one was open for 1% of the time, Pallas kernels for 0%

profile of v1, /device:TPU:0, one launch (start us, length us, event | category | flops | bytes accessed | tf_op | source)
XLA Modules:
  0.0 193.2 jit_solution(10056785791112799113)
XLA Ops:
  0.7 0.7 copy-done.1
  1.3 71.8 %all_gather.7 = f32[24,4096]{1,0:T(8,128)S(1)} all-gather(f32[24,128]{1,0:T(8,128)S(1)} %copy-done.1), channel_id=1, replica_groups=mesh['blade'=4,'inst'=4,'cell'=2] {'blade','inst','cell'}, dimensions={1}, use_global_device_ids=true | all-gather | bytes 405504 | tf_op jit(solution)/shard_map/all_gather | solution.py:79
  73.1 0.7 copy-done.2
  73.8 63.8 %all_gather.6 = f32[3,4096]{1,0:T(4,128)S(1)} all-gather(f32[3,128]{1,0:T(4,128)S(1)} %copy-done.2), channel_id=1, replica_groups=mesh['blade'=4,'inst'=4,'cell'=2] {'blade','inst','cell'}, dimensions={1}, use_global_device_ids=true | all-gather | bytes 50688 | tf_op jit(solution)/shard_map/all_gather | solution.py:80
  137.7 36.3 %while.12 = (s32[]{:T(128)}, f32[10,24,4,128]{3,1,2,0:T(8,128)S(1)}, s32[10,4,4]{2,1,0:T(4,128)S(1)}, f32[3,32,128]{2,0,1:T(4,128)S(1)}, f32[10,3,4,128]{3,2,0,1...) while((s32[]{:T(128)}, f32[10,24,4,128]{3,1,2,0:T(8,128)S(1)}, s32[10,4,4]{2,1,0:T(4,128)S(1)}, ...), condition=%wide.region_1.2_spmd, body=%wide.region_0.1_spmd.sunk | while | flops 79692848 | bytes 797209 | solution.py:61
  137.8 0.6 gather_fusion.1
  139.0 2.3 %fusion.80 = f32[10,24,4,128]{3,1,2,0:T(8,128)S(1)} fusion(f32[10,24,4,128]{3,1,2,0:T(8,128)S(1)} %get-tuple-element.176, s32[]{:T(128)} %get-tuple-element.175, f32[24,4,4,128]{3,0,2,1:T(8,128)S(1)} %bitcast.82, f32[4,128]{1,0:T(4,128)S(1)} %get-tuple-element.162, f32[4,4,128]{2,1,0:T(4,128)S(1)} %bitcast.92, f32[4,128]{1,0:T(4,128)S(1)} %get-tuple-element.164, ...), kind=kOutput, calls=%fused_computation.3.clone.1 | convolution fusion | flops 79691776 | bytes 276484 | tf_op jit(solution)/shard_map/while/body/eval_jaxpr/amkj,mkjc->amc/dot_general | solution.py:50
  141.4 0.6 gather_fusion.1
  142.6 2.3 %fusion.80 = f32[10,24,4,128]{3,1,2,0:T(8,128)S(1)} fusion(f32[10,24,4,128]{3,1,2,0:T(8,128)S(1)} %get-tuple-element.176, s32[]{:T(128)} %get-tuple-element.175, f32[24,4,4,128]{3,0,2,1:T(8,128)S(1)} %bitcast.82, f32[4,128]{1,0:T(4,128)S(1)} %get-tuple-element.162, f32[4,4,128]{2,1,0:T(4,128)S(1)} %bitcast.92, f32[4,128]{1,0:T(4,128)S(1)} %get-tuple-element.164, ...), kind=kOutput, calls=%fused_computation.3.clone.1 | convolution fusion | flops 79691776 | bytes 276484 | tf_op jit(solution)/shard_map/while/body/eval_jaxpr/amkj,mkjc->amc/dot_general | solution.py:50
  145.0 0.6 gather_fusion.1
  146.2 2.3 %fusion.80 = f32[10,24,4,128]{3,1,2,0:T(8,128)S(1)} fusion(f32[10,24,4,128]{3,1,2,0:T(8,128)S(1)} %get-tuple-element.176, s32[]{:T(128)} %get-tuple-element.175, f32[24,4,4,128]{3,0,2,1:T(8,128)S(1)} %bitcast.82, f32[4,128]{1,0:T(4,128)S(1)} %get-tuple-element.162, f32[4,4,128]{2,1,0:T(4,128)S(1)} %bitcast.92, f32[4,128]{1,0:T(4,128)S(1)} %get-tuple-element.164, ...), kind=kOutput, calls=%fused_computation.3.clone.1 | convolution fusion | flops 79691776 | bytes 276484 | tf_op jit(solution)/shard_map/while/body/eval_jaxpr/amkj,mkjc->amc/dot_general | solution.py:50
  148.7 0.6 gather_fusion.1
  149.9 2.3 %fusion.80 = f32[10,24,4,128]{3,1,2,0:T(8,128)S(1)} fusion(f32[10,24,4,128]{3,1,2,0:T(8,128)S(1)} %get-tuple-element.176, s32[]{:T(128)} %get-tuple-element.175, f32[24,4,4,128]{3,0,2,1:T(8,128)S(1)} %bitcast.82, f32[4,128]{1,0:T(4,128)S(1)} %get-tuple-element.162, f32[4,4,128]{2,1,0:T(4,128)S(1)} %bitcast.92, f32[4,128]{1,0:T(4,128)S(1)} %get-tuple-element.164, ...), kind=kOutput, calls=%fused_computation.3.clone.1 | convolution fusion | flops 79691776 | bytes 276484 | tf_op jit(solution)/shard_map/while/body/eval_jaxpr/amkj,mkjc->amc/dot_general | solution.py:50
  152.3 0.6 gather_fusion.1
  153.5 2.3 %fusion.80 = f32[10,24,4,128]{3,1,2,0:T(8,128)S(1)} fusion(f32[10,24,4,128]{3,1,2,0:T(8,128)S(1)} %get-tuple-element.176, s32[]{:T(128)} %get-tuple-element.175, f32[24,4,4,128]{3,0,2,1:T(8,128)S(1)} %bitcast.82, f32[4,128]{1,0:T(4,128)S(1)} %get-tuple-element.162, f32[4,4,128]{2,1,0:T(4,128)S(1)} %bitcast.92, f32[4,128]{1,0:T(4,128)S(1)} %get-tuple-element.164, ...), kind=kOutput, calls=%fused_computation.3.clone.1 | convolution fusion | flops 79691776 | bytes 276484 | tf_op jit(solution)/shard_map/while/body/eval_jaxpr/amkj,mkjc->amc/dot_general | solution.py:50
  155.9 0.6 gather_fusion.1
  157.1 2.3 %fusion.80 = f32[10,24,4,128]{3,1,2,0:T(8,128)S(1)} fusion(f32[10,24,4,128]{3,1,2,0:T(8,128)S(1)} %get-tuple-element.176, s32[]{:T(128)} %get-tuple-element.175, f32[24,4,4,128]{3,0,2,1:T(8,128)S(1)} %bitcast.82, f32[4,128]{1,0:T(4,128)S(1)} %get-tuple-element.162, f32[4,4,128]{2,1,0:T(4,128)S(1)} %bitcast.92, f32[4,128]{1,0:T(4,128)S(1)} %get-tuple-element.164, ...), kind=kOutput, calls=%fused_computation.3.clone.1 | convolution fusion | flops 79691776 | bytes 276484 | tf_op jit(solution)/shard_map/while/body/eval_jaxpr/amkj,mkjc->amc/dot_general | solution.py:50
  159.5 0.6 gather_fusion.1
  160.8 2.3 %fusion.80 = f32[10,24,4,128]{3,1,2,0:T(8,128)S(1)} fusion(f32[10,24,4,128]{3,1,2,0:T(8,128)S(1)} %get-tuple-element.176, s32[]{:T(128)} %get-tuple-element.175, f32[24,4,4,128]{3,0,2,1:T(8,128)S(1)} %bitcast.82, f32[4,128]{1,0:T(4,128)S(1)} %get-tuple-element.162, f32[4,4,128]{2,1,0:T(4,128)S(1)} %bitcast.92, f32[4,128]{1,0:T(4,128)S(1)} %get-tuple-element.164, ...), kind=kOutput, calls=%fused_computation.3.clone.1 | convolution fusion | flops 79691776 | bytes 276484 | tf_op jit(solution)/shard_map/while/body/eval_jaxpr/amkj,mkjc->amc/dot_general | solution.py:50
  163.2 0.6 gather_fusion.1
  164.4 2.3 %fusion.80 = f32[10,24,4,128]{3,1,2,0:T(8,128)S(1)} fusion(f32[10,24,4,128]{3,1,2,0:T(8,128)S(1)} %get-tuple-element.176, s32[]{:T(128)} %get-tuple-element.175, f32[24,4,4,128]{3,0,2,1:T(8,128)S(1)} %bitcast.82, f32[4,128]{1,0:T(4,128)S(1)} %get-tuple-element.162, f32[4,4,128]{2,1,0:T(4,128)S(1)} %bitcast.92, f32[4,128]{1,0:T(4,128)S(1)} %get-tuple-element.164, ...), kind=kOutput, calls=%fused_computation.3.clone.1 | convolution fusion | flops 79691776 | bytes 276484 | tf_op jit(solution)/shard_map/while/body/eval_jaxpr/amkj,mkjc->amc/dot_general | solution.py:50
  166.8 0.6 gather_fusion.1
  168.0 2.3 %fusion.80 = f32[10,24,4,128]{3,1,2,0:T(8,128)S(1)} fusion(f32[10,24,4,128]{3,1,2,0:T(8,128)S(1)} %get-tuple-element.176, s32[]{:T(128)} %get-tuple-element.175, f32[24,4,4,128]{3,0,2,1:T(8,128)S(1)} %bitcast.82, f32[4,128]{1,0:T(4,128)S(1)} %get-tuple-element.162, f32[4,4,128]{2,1,0:T(4,128)S(1)} %bitcast.92, f32[4,128]{1,0:T(4,128)S(1)} %get-tuple-element.164, ...), kind=kOutput, calls=%fused_computation.3.clone.1 | convolution fusion | flops 79691776 | bytes 276484 | tf_op jit(solution)/shard_map/while/body/eval_jaxpr/amkj,mkjc->amc/dot_general | solution.py:50
  170.4 0.6 gather_fusion.1
  171.6 2.3 %fusion.80 = f32[10,24,4,128]{3,1,2,0:T(8,128)S(1)} fusion(f32[10,24,4,128]{3,1,2,0:T(8,128)S(1)} %get-tuple-element.176, s32[]{:T(128)} %get-tuple-element.175, f32[24,4,4,128]{3,0,2,1:T(8,128)S(1)} %bitcast.82, f32[4,128]{1,0:T(4,128)S(1)} %get-tuple-element.162, f32[4,4,128]{2,1,0:T(4,128)S(1)} %bitcast.92, f32[4,128]{1,0:T(4,128)S(1)} %get-tuple-element.164, ...), kind=kOutput, calls=%fused_computation.3.clone.1 | convolution fusion | flops 79691776 | bytes 276484 | tf_op jit(solution)/shard_map/while/body/eval_jaxpr/amkj,mkjc->amc/dot_general | solution.py:50
  174.3 4.2 %collective-permute-done = f32[1,2,3,40,128]{4,3,2,1,0:T(8,128)S(1)} collective-permute-done((f32[1,2,3,40,128]{4,3,2,1,0:T(8,128)S(1)}, f32[1,2,3,40,128]{4,3,2,1,0:T(8,128)S(1)}, u32[]{:S(2)}, u32[]{:S(2)}) %collective-permute-start) | collective-permute-done | bytes 122912 | tf_op jit(solution)/shard_map/ppermute | solution.py:28
  178.7 0.6 fusion.32
  179.3 0.9 copy.32
  180.2 3.5 %all-to-all-start = ((f32[8,3,40,128]{3,2,1,0:T(8,128)}), f32[8,3,40,128]{3,2,1,0:T(8,128)S(1)}, u32[]{:S(2)}, u32[]{:S(2)}) async-start(f32[8,3,40,128]{3,2,1,0:T(8,128)} %copy.32), calls=%async_computation | async-start | bytes 983040 | tf_op jit(solution)/shard_map/all_to_all | solution.py:92
  183.7 0.8 copy_bitcast_fusion.1
  184.6 7.8 %all-to-all-done = f32[8,3,40,128]{3,2,1,0:T(8,128)S(1)} async-done(((f32[8,3,40,128]{3,2,1,0:T(8,128)}), f32[8,3,40,128]{3,2,1,0:T(8,128)S(1)}, u32[]{:S(2)}, u32[]{:S(2)}) %all-to-all-start) | async-done | bytes 491552 | tf_op jit(solution)/shard_map/all_to_all | solution.py:92
  192.4 0.8 copy.45
  (90 shorter events, 7.5 us)
Async XLA Ops:
  0.6 0.7 copy-start.1
  73.1 0.7 copy-start.2
  73.8 63.8 %copy-start.3 = (s32[40,1,4]{0,2,1:T(4,128)S(1)}, s32[40,1,4]{0,2,1:T(4,128)}, u32[]{:S(2)}) copy-start(s32[40,1,4]{0,2,1:T(4,128)} %param.9) | copy-start | bytes 1924
  73.8 63.9 %copy-start = (f32[3,40,128]{2,1,0:T(8,128)S(1)}, f32[3,40,128]{2,1,0:T(8,128)}, u32[]{:S(2)}) copy-start(f32[3,40,128]{2,1,0:T(8,128)} %param.6) | copy-start | bytes 184324
  174.2 4.4 %collective-permute-start = (f32[1,2,3,40,128]{4,3,2,1,0:T(8,128)S(1)}, f32[1,2,3,40,128]{4,3,2,1,0:T(8,128)S(1)}, u32[]{:S(2)}, u32[]{:S(2)}) collective-permute-start(f32[1,2,3,40,128]{4,3,2,1,0:T(8,128)S(1)} %constant_dynamic-slice_fusion.2), channel_id=1, source_target_pairs={{0,2},{2,4},{4,6},{6,0},{1,3},{3,5},{5,7},{7,1},{8,10},{10,12},{12... | collective-permute-start | bytes 368648 | tf_op jit(solution)/shard_map/ppermute | solution.py:28
  178.6 5.1 %collective-permute-start.1 = (f32[1,2,3,40,128]{4,3,2,1,0:T(8,128)S(1)}, f32[1,2,3,40,128]{4,3,2,1,0:T(8,128)S(1)}, u32[]{:S(2)}, u32[]{:S(2)}) collective-permute-start(f32[1,2,3,40,128]{4,3,2,1,0:T(8,128)S(1)} %get-tuple-element.117), channel_id=1, source_target_pairs={{0,4},{2,6},{4,0},{6,2},{1,5},{3,7},{5,1},{7,3},{8,12},{10,14},{12... | collective-permute-start | bytes 368648 | tf_op jit(solution)/shard_map/ppermute | solution.py:28
  178.6 5.1 %collective-permute-start.2 = (f32[1,2,3,40,128]{4,3,2,1,0:T(8,128)S(1)}, f32[1,2,3,40,128]{4,3,2,1,0:T(8,128)S(1)}, u32[]{:S(2)}, u32[]{:S(2)}) collective-permute-start(f32[1,2,3,40,128]{4,3,2,1,0:T(8,128)S(1)} %get-tuple-element.116), channel_id=1, source_target_pairs={{0,6},{2,0},{4,2},{6,4},{1,7},{3,1},{5,3},{7,5},{8,14},{10,8},{12,... | collective-permute-start | bytes 368648 | tf_op jit(solution)/shard_map/ppermute | solution.py:28
  180.2 12.2 %all-to-all-start = ((f32[8,3,40,128]{3,2,1,0:T(8,128)}), f32[8,3,40,128]{3,2,1,0:T(8,128)S(1)}, u32[]{:S(2)}, u32[]{:S(2)}) async-start(f32[8,3,40,128]{3,2,1,0:T(8,128)} %copy.32), calls=%async_computation | async-start | bytes 983040 | tf_op jit(solution)/shard_map/all_to_all | solution.py:92
